TPU v7x, 256 devices: a whole 4x4x8 slice. The times are simulated.
256 devices in a mesh: inp: 4 (over y_hi, core), dep: 8 (over x, y_lo), out: 8 (over z).
Axes of the slice: x: 4, y: 4 (y_hi: 2, y_lo: 2; y = y_hi * 2 + y_lo), z: 8, core: 2. Of those that a mesh axis runs over, the one named last changes fastest.
Arguments:
- tokens: bfloat16 [1024, 16384], P('inp', 'out'), may hold values from -6 to 6
- gate_up_weight: bfloat16 [16384, 2, 28672], P('out', None, ('inp', 'dep')), may hold values from -0.046875 to 0.046875
- down_weight: bfloat16 [28672, 16384], P(('inp', 'dep'), 'out'), may hold values from -0.03125 to 0.03125
Outputs:
- layer_output: bfloat16 [1024, 16384], P(('inp', 'dep'), 'out')
All inputs are finite; a program needn't handle non-finite values.
Results may differ from a plain program's by a relative error of at most 0.0049.
Values may be sent and summed in bfloat16 or wider, within the bound.
A program may use at most 128 MiB of HBM per device.

v0:
```python
import jax
import jax.numpy as jnp
from jax import lax
from jax.sharding import PartitionSpec as P


def swiglu(projected):
    return (jax.nn.silu(projected[:, 0, :]) * projected[:, 1, :]).astype(jnp.bfloat16)


def shards(tokens, gate_up_weight, down_weight):
    local_width = gate_up_weight.shape[0]
    block_units = gate_up_weight.shape[2]
    flat_weight = gate_up_weight.reshape(local_width, 2 * block_units)
    projected = jnp.dot(
        lax.all_gather(tokens, "inp", axis=0, tiled=True),
        flat_weight,
        preferred_element_type=jnp.float32,
    )
    projected = projected.reshape(projected.shape[0], 2, block_units)
    totals = lax.psum(projected, "out")
    full_hidden = swiglu(totals)
    result = lax.psum_scatter(
        jnp.dot(full_hidden, down_weight, preferred_element_type=jnp.float32),
        ("inp", "dep"),
        scatter_dimension=0,
        tiled=True,
    )
    return result.astype(jnp.bfloat16)


def solution(mesh):
    placed = (P("inp", "out"), P("out", None, ("inp", "dep")), P(("inp", "dep"), "out"))
    return jax.shard_map(
        shards, mesh=mesh, in_specs=placed, out_specs=P(("inp", "dep"), "out"), check_vma=False
    )
```

profile of v0, /device:TPU:10, one launch (start us, length us, event | category | flops | bytes accessed | tf_op | source)
XLA Modules:
  0.0 443.8 jit_solution(10383628695858579418)
XLA Ops:
  6.5 0.0 all-gather.2.cloned.1.call-start
  6.5 0.7 all-gather.2.cloned.1.call-update
  7.3 0.0 all-reduce.2.cloned.1.call-start
  7.3 7.6 %copy.5 = bf16[256,8,2,896]{3,1,2,0:T(8,128)(2,1)} copy(bf16[256,8,2,896]{3,2,1,0:T(2,128)(2,1)} %bitcast.23) | data formatting | bytes 14680064
  14.9 10.5 %copy.4 = bf16[1792,2048]{1,0:T(8,128)(2,1)} copy(bf16[1792,2048]{0,1:T(8,128)(2,1)} %bitcast.22) | data formatting | bytes 14680064 | tf_op jit(solution)/shard_map/dot_general | solution.py:15
  25.4 26.8 %all-gather.2.cloned.1.call-done = bf16[1024,2048]{1,0:T(8,128)(2,1)} async-done(((bf16[256,2048]{1,0:T(8,128)(2,1)}), bf16[1024,2048]{1,0:T(8,128)(2,1)}) %all-gather.2.cloned.1.call-update) | async-done | bytes 4194320 | tf_op jit(solution)/shard_map/all_gather | solution.py:16
  52.3 14.3 %fusion = f32[1024,2,896]{2,0,1:T(8,128)} fusion(bf16[2,896,2048]{2,1,0:T(8,128)(2,1)} %bitcast.24, bf16[1024,2048]{1,0:T(8,128)(2,1)} %all-gather.2.cloned.1.call-done), kind=kOutput, calls=%fused_computation | convolution fusion | flops 7516192768 | bytes 18874368 | tf_op jit(solution)/shard_map/dot_general | solution.py:15
  66.5 0.0 all-reduce.2.cloned.1.call-update
  66.6 0.0 reduce-scatter.2.cloned.1.call-start
  66.6 168.7 %all-reduce.2.cloned.1.call-done = f32[1024,2,896]{2,0,1:T(8,128)} async-done(((f32[1024,2,896]{2,0,1:T(8,128)}), f32[1024,2,896]{2,0,1:T(8,128)}) %all-reduce.2.cloned.1.call-update) | async-done | bytes 7340048 | tf_op jit(solution)/shard_map/psum | solution.py:21
  235.3 11.9 %fusion.4 = f32[1024,2048]{1,0:T(8,128)} fusion(bf16[896,2048]{1,0:T(8,128)(2,1)} %param.5, f32[1024,2,896]{2,0,1:T(8,128)} %all-reduce.2.cloned.1.call-done), kind=kOutput, calls=%fused_computation.6 | convolution fusion | flops 3763601408 | bytes 19398656 | tf_op jit(solution)/shard_map/dot_general | solution.py:24
  247.3 0.0 reduce-scatter.2.cloned.1.call-update
  247.3 188.3 %reduce-scatter.2.cloned.1.call-done = f32[32,2048]{1,0:T(8,128)} async-done(((f32[1024,2048]{1,0:T(8,128)}), f32[32,2048]{1,0:T(8,128)}) %reduce-scatter.2.cloned.1.call-update) | async-done | bytes 262160 | tf_op jit(solution)/shard_map/reduce_scatter | solution.py:23
  435.6 1.6 convert_element_type.7
Async XLA Ops:
  6.5 45.7 %all-gather.2.cloned.1.call-start = ((), (), s32[]{:S(2)}) async-start(), calls=%async_computation.1 | async-start | bytes 5242880 | tf_op jit(solution)/shard_map/all_gather | solution.py:16
  7.3 228.1 %all-reduce.2.cloned.1.call-start = ((), (), s32[]{:S(2)}) async-start(), calls=%async_computation.2 | async-start | bytes 14680064 | tf_op jit(solution)/shard_map/psum | solution.py:21
  66.6 369.1 %reduce-scatter.2.cloned.1.call-start = ((), (), s32[]{:S(2)}) async-start(), calls=%async_computation.3 | async-start | bytes 8650752 | tf_op jit(solution)/shard_map/reduce_scatter | solution.py:23
Sparse Core Ops, SparseCore 0:
  9.2 43.0 all-gather.1
  66.7 168.5 all-reduce.1
  247.4 188.1 reduce-scatter.1
where the time goes:
time: 444 us
  waiting for transfers between devices  385 us (87%)
  matrix products  26.2 us (6%)
  local copies, waits for them, and re-layouts  18.1 us (4%)
  between operations  13.1 us (3%)
    reduce_scatter x1, waiting for transfers between devices, shards(): lax.psum_scatter(jnp.dot(full_hidden, down_weight, preferred_element_type...  188 us
    psum x1, waiting for transfers between devices, shards(): totals = lax.psum(projected, 'out')  169 us
    all_gather x1, waiting for transfers between devices, shards(): lax.all_gather(tokens, 'inp', axis=0, tiled=True)  26.8 us
    dot_general x1, matrix products, shards(): jnp.dot(lax.all_gather(tokens, 'inp', axis=0, tiled=True), flat_weight, p...  14.3 us
    dot_general x1, matrix products, shards(): jnp.dot(full_hidden, down_weight, preferred_element_type=jnp.float32)  11.9 us
    dot_general x1, local copies, waits for them, and re-layouts, shards(): jnp.dot(lax.all_gather(tokens, 'inp', axis=0, tiled=True), flat_weight, p...  10.5 us
  transfers between devices with their start and end apart: 3, of which 3 were waited for; matrix products, arithmetic and copies ran while one was open for 4% of the time, Pallas kernels for 0%

commit v1 on v0

--- a/solution.py
+++ b/solution.py
@@ -1,7 +1,20 @@
+import functools
 import jax
 import jax.numpy as jnp
 from jax import lax
 from jax.sharding import PartitionSpec as P
+
+
+def group_shelves(local, named_axis):
+    return jnp.concatenate(
+        lax.all_to_all(
+            jnp.stack(tuple((local for _ in range(lax.axis_size(named_axis))))), named_axis, 0, 0
+        ),
+        axis=0,
+    )
+
+
+render_the_field = functools.partial(group_shelves, named_axis="inp")
 
 
 def swiglu(projected):
@@ -12,11 +25,7 @@
     local_width = gate_up_weight.shape[0]
     block_units = gate_up_weight.shape[2]
     flat_weight = gate_up_weight.reshape(local_width, 2 * block_units)
-    projected = jnp.dot(
-        lax.all_gather(tokens, "inp", axis=0, tiled=True),
-        flat_weight,
-        preferred_element_type=jnp.float32,
-    )
+    projected = jnp.dot(render_the_field(tokens), flat_weight, preferred_element_type=jnp.float32)
     projected = projected.reshape(projected.shape[0], 2, block_units)
     totals = lax.psum(projected, "out")
     full_hidden = swiglu(totals)

time: 444 us -> 458 us (1.032)
  starting transfers between devices: 0.08 us -> 4.95 us
    all_to_all x0 -> x1, waiting for transfers between devices: none -> 31.5 us  [group_shelves(): lax.all_to_all(jnp.stack(tuple((local for _ in range(lax.axis_size(named_...]
    all_gather x1 -> x0, waiting for transfers between devices: 26.8 us -> none  [shards(): lax.all_gather(tokens, 'inp', axis=0, tiled=True)]
    all_to_all x0 -> x1, starting transfers between devices: none -> 4.87 us  [group_shelves(): lax.all_to_all(jnp.stack(tuple((local for _ in range(lax.axis_size(named_...]
where the time goes in v1:
time: 458 us
  waiting for transfers between devices  389 us (85%)
  matrix products  26.2 us (6%)
  local copies, waits for them, and re-layouts  21.9 us (5%)
  between operations  13.4 us (3%)
  starting transfers between devices  4.95 us (1%)
    reduce_scatter x1, waiting for transfers between devices, shards(): lax.psum_scatter(jnp.dot(full_hidden, down_weight, preferred_element_type...  188 us
    psum x1, waiting for transfers between devices, shards(): totals = lax.psum(projected, 'out')  170 us
    all_to_all x1, waiting for transfers between devices, group_shelves(): lax.all_to_all(jnp.stack(tuple((local for _ in range(lax.axis_size(named_...  31.5 us
    dot_general x1, matrix products, shards(): jnp.dot(render_the_field(tokens), flat_weight, preferred_element_type=jnp...  14.3 us
    dot_general x1, matrix products, shards(): jnp.dot(full_hidden, down_weight, preferred_element_type=jnp.float32)  11.9 us
    dot_general x1, local copies, waits for them, and re-layouts, shards(): jnp.dot(render_the_field(tokens), flat_weight, preferred_element_type=jnp...  10.5 us
  transfers between devices with their start and end apart: 3, of which 3 were waited for; matrix products, arithmetic and copies ran while one was open for 4% of the time, Pallas kernels for 0%

profile of v1, /device:TPU:10, one launch (start us, length us, event | category | flops | bytes accessed | tf_op | source)
XLA Modules:
  0.0 457.6 jit_solution(18367404070961263274)
XLA Ops:
  6.5 3.8 stack.2
  10.3 4.9 %all-to-all-start = ((bf16[4,256,2048]{2,1,0:T(8,128)(2,1)}), bf16[4,256,2048]{2,1,0:T(8,128)(2,1)}, u32[]{:S(2)}, u32[]{:S(2)}) async-start(bf16[4,256,2048]{2,1,0:T(8,128)(2,1)} %stack.2), calls=%async_computation | async-start | bytes 8388608 | tf_op jit(solution)/shard_map/all_to_all | solution.py:10
  15.2 0.0 all-reduce.2.cloned.1.call-start
  15.2 7.6 %copy.5 = bf16[256,8,2,896]{3,1,2,0:T(8,128)(2,1)} copy(bf16[256,8,2,896]{3,2,1,0:T(2,128)(2,1)} %bitcast.24) | data formatting | bytes 14680064
  22.8 10.5 %copy.4 = bf16[1792,2048]{1,0:T(8,128)(2,1)} copy(bf16[1792,2048]{0,1:T(8,128)(2,1)} %bitcast.23) | data formatting | bytes 14680064 | tf_op jit(solution)/shard_map/dot_general | solution.py:28
  33.4 31.5 %all-to-all-done = bf16[4,256,2048]{2,1,0:T(8,128)(2,1)} async-done(((bf16[4,256,2048]{2,1,0:T(8,128)(2,1)}), bf16[4,256,2048]{2,1,0:T(8,128)(2,1)}, u32[]{:S(2)}, u32[]{:S(2)}) %all-to-all-start) | async-done | bytes 4194336 | tf_op jit(solution)/shard_map/all_to_all | solution.py:10
  64.9 14.3 %fusion.6 = f32[1024,2,896]{2,0,1:T(8,128)} fusion(bf16[1024,2048,1]{1,0,2:T(8,128)(2,1)} %bitcast.1, bf16[2,896,2048]{2,1,0:T(8,128)(2,1)} %bitcast.25), kind=kOutput, calls=%fused_computation.7 | convolution fusion | flops 7516192768 | bytes 18874368 | tf_op jit(solution)/shard_map/dot_general | solution.py:28
  79.2 0.0 all-reduce.2.cloned.1.call-update
  79.2 0.0 reduce-scatter.2.cloned.1.call-start
  79.3 169.6 %all-reduce.2.cloned.1.call-done = f32[1024,2,896]{2,0,1:T(8,128)} async-done(((f32[1024,2,896]{2,0,1:T(8,128)}), f32[1024,2,896]{2,0,1:T(8,128)}) %all-reduce.2.cloned.1.call-update) | async-done | bytes 7340048 | tf_op jit(solution)/shard_map/psum | solution.py:30
  248.9 11.9 %fusion.2 = f32[1024,2048]{1,0:T(8,128)} fusion(bf16[896,2048]{1,0:T(8,128)(2,1)} %param.5, f32[1024,2,896]{2,0,1:T(8,128)} %all-reduce.2.cloned.1.call-done), kind=kOutput, calls=%fused_computation.4 | convolution fusion | flops 3763601408 | bytes 19398656 | tf_op jit(solution)/shard_map/dot_general | solution.py:33
  260.8 0.0 reduce-scatter.2.cloned.1.call-update
  260.9 188.2 %reduce-scatter.2.cloned.1.call-done = f32[32,2048]{1,0:T(8,128)} async-done(((f32[1024,2048]{1,0:T(8,128)}), f32[32,2048]{1,0:T(8,128)}) %reduce-scatter.2.cloned.1.call-update) | async-done | bytes 262160 | tf_op jit(solution)/shard_map/reduce_scatter | solution.py:32
  449.1 1.6 convert_element_type.7
Async XLA Ops:
  10.3 54.6 %all-to-all-start = ((bf16[4,256,2048]{2,1,0:T(8,128)(2,1)}), bf16[4,256,2048]{2,1,0:T(8,128)(2,1)}, u32[]{:S(2)}, u32[]{:S(2)}) async-start(bf16[4,256,2048]{2,1,0:T(8,128)(2,1)} %stack.2), calls=%async_computation | async-start | bytes 8388608 | tf_op jit(solution)/shard_map/all_to_all | solution.py:10
  15.2 233.7 %all-reduce.2.cloned.1.call-start = ((), (), s32[]{:S(2)}) async-start(), calls=%async_computation.2 | async-start | bytes 14680064 | tf_op jit(solution)/shard_map/psum | solution.py:30
  79.2 369.9 %reduce-scatter.2.cloned.1.call-start = ((), (), s32[]{:S(2)}) async-start(), calls=%async_computation.3 | async-start | bytes 8650752 | tf_op jit(solution)/shard_map/reduce_scatter | solution.py:32
Sparse Core Ops, SparseCore 0:
  79.3 169.5 all-reduce.1
  261.0 188.0 reduce-scatter.1
